TPU v7x, 32 devices: a whole 2x2x4 slice. The times are simulated.
32 devices in a mesh: sect: 4 (over y, x), tile: 8 (over z, core).
Axes of the slice: x: 2, y: 2, z: 4, core: 2. Of those that a mesh axis runs over, the one named last changes fastest.
Arguments:
- zonal: float32 [4, 64, 512], P('sect', 'tile'), may hold values from -1.5 to 1.5
- merid: float32 [4, 64, 512], P('sect', 'tile'), may hold values from -1.5 to 1.5
- height: float32 [4, 64, 512], P('sect', 'tile'), may hold values from -6 to 6
- level_kappa: float32 [4], replicated, may hold values from 0.2 to 2
- sea: int32 [64, 512], P('tile'), may hold values 0 or 1
- flags: int32 [4, 64, 512], P(None, 'tile', 'sect'), may hold values 0 or 1
- conc: float32 [12, 4, 64, 512], P(None, None, 'tile', 'sect'), may hold values from 0.1 to 2
- react: float32 [12, 12], replicated, may hold values from -1.2 to 1.2
- absorb: float32 [12], replicated, may hold values from 0.05 to 1
- light: float32 [4], replicated, may hold values from 0.1 to 1
Outputs:
- conc_out: float32 [12, 4, 64, 512], P(None, None, 'tile', 'sect')
- zonal_out: float32 [4, 64, 512], P('sect', 'tile')
- merid_out: float32 [4, 64, 512], P('sect', 'tile')
- height_out: float32 [4, 64, 512], P('sect', 'tile')
All inputs are finite; a program needn't handle non-finite values. No bound on the sum of `sea` or of `flags` on one device may be relied on, other than what follows from the above.
Results may differ from a plain program's by a relative error of at most 0.00022.
Values sent between devices are 32-bit elements; how exact they have to be, the bound alone decides.
A program may use at most 64 MiB of HBM per device.

v0:
```python
import jax
import jax.numpy as jnp
from jax import lax
from jax.sharding import PartitionSpec as P

STEPS = 4
INTERVALS = 2


time_step = 0.1
gravity = 1.0
coriolis = 0.3
viscosity = 0.05
heat_coupling = 0.05
tracer_step = 0.5
stir_gain = 4.0


def padded_2(cells, sides, width):
    for axis, dim in sides:
        count = lax.axis_size(axis)
        head = lax.slice_in_dim(cells, 0, width, axis=dim)
        tail = lax.slice_in_dim(cells, cells.shape[dim] - width, cells.shape[dim], axis=dim)
        cells = jnp.concatenate(
            [
                lax.ppermute(tail, axis, [(i, (i + 1) % count) for i in range(count)]),
                cells,
                lax.ppermute(head, axis, [((i + 1) % count, i) for i in range(count)]),
            ],
            axis=dim,
        )
    return cells


def along_x(field):
    return 0.5 * (jnp.roll(field, -1, 2) - jnp.roll(field, 1, 2))


def along_y(padded):
    return 0.5 * (padded[:, 2:] - padded[:, :-2])


def laplace(field, padded):
    total = padded[:, 2:] + padded[:, :-2]
    total = total + jnp.roll(field, -1, 2) + jnp.roll(field, 1, 2)
    return total - 4.0 * field


def upwind(centre, ahead, behind, speed, flag):
    upper = jnp.maximum(speed, 0.0) * (centre - behind) + jnp.minimum(speed, 0.0) * (ahead - centre)
    middle = 0.5 * speed * (ahead - behind)
    return jnp.where(flag == 1, upper, middle)


def column_solve(starred, kappa):
    levels = starred.shape[1]
    couple = [tracer_step * 0.5 * (kappa[k] + kappa[k + 1]) for k in range(levels - 1)]
    factor = []
    partial_rhs = []
    for k in range(levels):
        lower = couple[k - 1] if k > 0 else jnp.zeros_like(kappa[0])
        upper = couple[k] if k < levels - 1 else jnp.zeros_like(kappa[0])
        diagonal = 1.0 + lower + upper
        if k == 0:
            denom = diagonal
            rhs_now = starred[:, 0] / denom
        else:
            denom = diagonal + lower * factor[k - 1]
            rhs_now = (starred[:, k] + lower * partial_rhs[k - 1]) / denom
        factor.append(-upper / denom)
        partial_rhs.append(rhs_now)
    result = [None] * levels
    result[levels - 1] = partial_rhs[levels - 1]
    for k in range(levels - 2, -1, -1):
        result[k] = partial_rhs[k] - factor[k] * result[k + 1]
    return jnp.stack(result, axis=1)


def body(zonal, merid, height, level_kappa, sea, flags, conc, react, absorb, light):
    sect_index = lax.axis_index("sect")
    levels_dev = zonal.shape[0]
    column_dev = conc.shape[3]
    wet_rows = sea.astype(jnp.float32)
    wet_cols = lax.dynamic_slice_in_dim(wet_rows, sect_index * column_dev, column_dev, 1)
    own_kappa = lax.dynamic_slice_in_dim(level_kappa, sect_index * levels_dev, levels_dev, 0)
    forcing = jnp.zeros(height.shape, jnp.float32)
    for interval in range(INTERVALS):
        zonal_sum = jnp.zeros(zonal.shape, jnp.float32)
        merid_sum = jnp.zeros(merid.shape, jnp.float32)
        for step in range(STEPS):
            forced = height + time_step * heat_coupling * forcing
            wide = padded_2(jnp.stack([zonal, merid, forced]), (("tile", 2),), 2)
            zonal_wide = wide[0]
            merid_wide = wide[1]
            forced_wide = wide[2]
            zonal_pad = zonal_wide[:, 1:-1]
            merid_pad = merid_wide[:, 1:-1]
            height_ext = forced_wide[:, 1:-1] - time_step * (
                along_x(zonal_pad) + along_y(merid_wide)
            )
            height = height_ext[:, 1:-1]
            zonal_new = wet_rows * (
                zonal
                + time_step
                * (
                    coriolis * merid
                    - gravity * along_x(height)
                    + viscosity * laplace(zonal, zonal_pad)
                )
            )
            merid_new = wet_rows * (
                merid
                + time_step
                * (
                    -coriolis * zonal
                    - gravity * along_y(height_ext)
                    + viscosity * laplace(merid, merid_pad)
                )
            )
            zonal, merid = (zonal_new, merid_new)
            zonal_sum = zonal_sum + zonal
            merid_sum = merid_sum + merid
        zonal_mean = zonal_sum / STEPS
        merid_mean = merid_sum / STEPS
        kappa_rows = own_kappa[:, None, None] * (
            1.0 + stir_gain * (zonal_mean * zonal_mean + merid_mean * merid_mean)
        )
        arrived = lax.all_to_all(
            jnp.stack([zonal_mean, merid_mean, kappa_rows]),
            "sect",
            split_axis=3,
            concat_axis=1,
            tiled=True,
        )
        zonal_cols = arrived[0]
        merid_cols = arrived[1]
        kappa_cols = arrived[2]
        padded = padded_2(conc, (("tile", 2), ("sect", 3)), 1)
        east = padded[:, :, 1:-1, 2:]
        west = padded[:, :, 1:-1, :-2]
        north = padded[:, :, 2:, 1:-1]
        south = padded[:, :, :-2, 1:-1]
        moving_terms = upwind(conc, east, west, zonal_cols, flags) + upwind(
            conc, north, south, merid_cols, flags
        )
        starred = conc - tracer_step * wet_cols * moving_terms
        mixed = column_solve(starred, kappa_cols)
        growth = jnp.einsum("ij,jzyx->izyx", react, mixed, precision=lax.Precision.HIGHEST)
        conc = mixed + tracer_step * wet_cols * growth
        if interval + 1 < INTERVALS:
            heat_cols = light[:, None, None] * jnp.einsum(
                "k,kzyx->zyx", absorb, conc, precision=lax.Precision.HIGHEST
            )
            forcing = lax.all_to_all(heat_cols, "sect", split_axis=0, concat_axis=2, tiled=True)
    return (conc, zonal, merid, height)


def solution(mesh):
    placed = (
        P("sect", "tile", None),
        P("sect", "tile", None),
        P("sect", "tile", None),
        P(),
        P("tile", None),
        P(None, "tile", "sect"),
        P(None, None, "tile", "sect"),
        P(),
        P(),
        P(),
    )
    return jax.shard_map(
        body,
        mesh=mesh,
        in_specs=placed,
        out_specs=(
            P(None, None, "tile", "sect"),
            P("sect", "tile", None),
            P("sect", "tile", None),
            P("sect", "tile", None),
        ),
        check_vma=False,
    )
```

profile of v0, /device:TPU:0, one launch (start us, length us, event | category | flops | bytes accessed | tf_op | source)
XLA Modules:
  0.0 116.7 jit_solution(4213536475629891333)
XLA Ops:
  0.6 0.8 pad_maximum_fusion.46
  1.5 0.5 collective-permute-start
  2.0 4.1 %collective-permute-start.1 = (f32[3,1,2,512]{3,2,1,0:T(2,128)S(1)}, f32[3,1,2,512]{3,2,1,0:T(2,128)S(1)}, u32[]{:S(2)}, u32[]{:S(2)}) collective-permute-start(f32[3,1,2,512]{3,2,1,0:T(2,128)S(1)} %get-tuple-element.119), channel_id=1, source_target_pairs={{1,0},{2,1},{3,2},{4,3},{5,4},{6,5},{7,6},{0,7},{9,8},{10,9},{11,1... | collective-permute-start | bytes 36872 | tf_op jit(solution)/shard_map/ppermute | solution.py:28
  6.1 1.0 copy.503
  7.2 3.5 %collective-permute-start.9 = (f32[12,4,1,128]{3,0,2,1:T(8,128)S(1)}, f32[12,4,1,128]{3,0,2,1:T(8,128)S(1)}, u32[]{:S(2)}, u32[]{:S(2)}) collective-permute-start(f32[12,4,1,128]{3,0,2,1:T(8,128)S(1)} %get-tuple-element.67), channel_id=1, source_target_pairs={{1,0},{2,1},{3,2},{4,3},{5,4},{6,5},{7,6},{0,7},{9,8},{10,9},{11,1... | collective-permute-start | bytes 73736 | tf_op jit(solution)/shard_map/ppermute | solution.py:28
  10.9 0.6 copy-done.4
  11.7 0.6 copy-done.1
  12.4 0.7 copy-done.8
  13.1 0.6 copy-done.11
  13.8 0.7 dynamic_slice.7
  15.4 3.5 %collective-permute-start.3 = (f32[3,1,2,512]{3,2,1,0:T(2,128)S(1)}, f32[3,1,2,512]{3,2,1,0:T(2,128)S(1)}, u32[]{:S(2)}, u32[]{:S(2)}) collective-permute-start(f32[3,1,2,512]{3,2,1,0:T(2,128)S(1)} %get-tuple-element.117), channel_id=1, source_target_pairs={{1,0},{2,1},{3,2},{4,3},{5,4},{6,5},{7,6},{0,7},{9,8},{10,9},{11,1... | collective-permute-start | bytes 36872 | tf_op jit(solution)/shard_map/ppermute | solution.py:28
  19.0 1.3 %collective-permute-done.2 = f32[3,1,2,512]{3,2,1,0:T(2,128)S(1)} collective-permute-done((f32[3,1,2,512]{3,2,1,0:T(2,128)S(1)}, f32[3,1,2,512]{3,2,1,0:T(2,128)S(1)}, u32[]{:S(2)}, u32[]{:S(2)}) %collective-permute-start.2) | collective-permute-done | bytes 12320 | tf_op jit(solution)/shard_map/ppermute | solution.py:26
  21.2 3.6 %collective-permute-start.5 = (f32[3,1,2,512]{3,2,1,0:T(2,128)S(1)}, f32[3,1,2,512]{3,2,1,0:T(2,128)S(1)}, u32[]{:S(2)}, u32[]{:S(2)}) collective-permute-start(f32[3,1,2,512]{3,2,1,0:T(2,128)S(1)} %get-tuple-element.115), channel_id=1, source_target_pairs={{1,0},{2,1},{3,2},{4,3},{5,4},{6,5},{7,6},{0,7},{9,8},{10,9},{11,1... | collective-permute-start | bytes 36872 | tf_op jit(solution)/shard_map/ppermute | solution.py:28
  25.0 0.6 copy-done.5
  25.6 0.9 fusion.259
  26.5 1.9 %collective-permute-start.10 = (f32[12,4,10,1]{3,0,2,1:T(8,128)}, f32[12,4,10,1]{3,0,2,1:T(8,128)S(1)}, u32[]{:S(2)}, u32[]{:S(2)}) collective-permute-start(f32[12,4,10,1]{3,0,2,1:T(8,128)} %get-tuple-element.62), channel_id=1, source_target_pairs={{0,8},{8,16},{16,24},{24,0},{1,9},{9,17},{17,25},{25,1},{2,10},{10... | collective-permute-start | bytes 5768 | tf_op jit(solution)/shard_map/ppermute | solution.py:26
  28.5 1.0 collective-permute-start.11
  30.2 3.5 %collective-permute-start.7 = (f32[3,1,2,512]{3,2,1,0:T(2,128)S(1)}, f32[3,1,2,512]{3,2,1,0:T(2,128)S(1)}, u32[]{:S(2)}, u32[]{:S(2)}) collective-permute-start(f32[3,1,2,512]{3,2,1,0:T(2,128)S(1)} %get-tuple-element.113), channel_id=1, source_target_pairs={{1,0},{2,1},{3,2},{4,3},{5,4},{6,5},{7,6},{0,7},{9,8},{10,9},{11,1... | collective-permute-start | bytes 36872 | tf_op jit(solution)/shard_map/ppermute | solution.py:28
  33.8 1.3 %collective-permute-done.6 = f32[3,1,2,512]{3,2,1,0:T(2,128)S(1)} collective-permute-done((f32[3,1,2,512]{3,2,1,0:T(2,128)S(1)}, f32[3,1,2,512]{3,2,1,0:T(2,128)S(1)}, u32[]{:S(2)}, u32[]{:S(2)}) %collective-permute-start.6) | collective-permute-done | bytes 12320 | tf_op jit(solution)/shard_map/ppermute | solution.py:26
  35.6 0.8 multiply_bitcast_fusion.5
  36.4 0.8 copy.490
  37.3 0.5 broadcast.650
  37.8 3.3 %reduce = f32[512,3,8]{2,1,0:T(4,128)S(1)} reduce(f32[512,3,1,8]{3,2,1,0:T(1,128)S(1)} %bitcast.205, f32[]{:T(128)} %broadcast.650), dimensions={2}, to_apply=%bitcast.189.reduce_sub_computation | reduce | bytes 98308
  41.1 1.3 %reshape.1284 = f32[4,1,3072]{2,1,0:T(1,128)} reshape(f32[512,3,8]{2,1,0:T(4,128)S(1)} %reduce) | data formatting | bytes 98304
  42.4 3.3 %all-to-all-start = ((f32[4,1,3072]{2,1,0:T(1,128)}), f32[4,1,3072]{2,1,0:T(1,128)S(1)}, u32[]{:S(2)}, u32[]{:S(2)}) async-start(f32[4,1,3072]{2,1,0:T(1,128)} %reshape.1284), calls=%async_computation | async-start | bytes 98304 | tf_op jit(solution)/shard_map/all_to_all | solution.py:128
  45.9 4.6 %all-to-all-done = f32[4,1,3072]{2,1,0:T(1,128)S(1)} async-done(((f32[4,1,3072]{2,1,0:T(1,128)}), f32[4,1,3072]{2,1,0:T(1,128)S(1)}, u32[]{:S(2)}, u32[]{:S(2)}) %all-to-all-start) | async-done | bytes 49184 | tf_op jit(solution)/shard_map/all_to_all | solution.py:128
  50.4 0.8 reduce.1
  51.2 1.2 %reshape.1285 = f32[512,3,1,8]{3,2,1,0:T(1,128)S(1)} reshape(f32[4,3072]{1,0:T(4,128)S(1)} %reduce.1) | data formatting | bytes 98304
  52.5 0.9 copy.491
  53.4 0.7 copy-done.6
  54.1 0.4 fusion.21
  54.6 0.4 fusion.3
  55.0 0.3 copy-done.9
  55.3 0.3 fusion.244
  55.6 0.6 copy-done.10
  56.2 0.7 broadcast_multiply_fusion
  56.9 3.3 %all-to-all-start.1 = ((f32[4,8,128]{2,1,0:T(8,128)}), f32[4,8,128]{2,1,0:T(8,128)S(1)}, u32[]{:S(2)}, u32[]{:S(2)}) async-start(f32[4,8,128]{2,1,0:T(8,128)} %broadcast_multiply_fusion), calls=%async_computation.1 | async-start | bytes 32768 | tf_op jit(solution)/shard_map/all_to_all | solution.py:154
  60.2 4.6 %all-to-all-done.1 = f32[4,8,128]{2,1,0:T(8,128)S(1)} async-done(((f32[4,8,128]{2,1,0:T(8,128)}), f32[4,8,128]{2,1,0:T(8,128)S(1)}, u32[]{:S(2)}, u32[]{:S(2)}) %all-to-all-start.1) | async-done | bytes 16416 | tf_op jit(solution)/shard_map/all_to_all | solution.py:154
  64.9 3.5 %collective-permute-start.13 = (f32[3,1,2,512]{3,2,1,0:T(2,128)S(1)}, f32[3,1,2,512]{3,2,1,0:T(2,128)S(1)}, u32[]{:S(2)}, u32[]{:S(2)}) collective-permute-start(f32[3,1,2,512]{3,2,1,0:T(2,128)S(1)} %get-tuple-element.105), channel_id=1, source_target_pairs={{1,0},{2,1},{3,2},{4,3},{5,4},{6,5},{7,6},{0,7},{9,8},{10,9},{11,1... | collective-permute-start | bytes 36872 | tf_op jit(solution)/shard_map/ppermute | solution.py:28
  68.5 3.5 %collective-permute-start.21 = (f32[12,4,1,128]{3,0,2,1:T(8,128)S(1)}, f32[12,4,1,128]{3,0,2,1:T(8,128)S(1)}, u32[]{:S(2)}, u32[]{:S(2)}) collective-permute-start(f32[12,4,1,128]{3,0,2,1:T(8,128)S(1)} %get-tuple-element.65), channel_id=1, source_target_pairs={{1,0},{2,1},{3,2},{4,3},{5,4},{6,5},{7,6},{0,7},{9,8},{10,9},{11,1... | collective-permute-start | bytes 73736 | tf_op jit(solution)/shard_map/ppermute | solution.py:28
  73.0 3.5 %collective-permute-start.15 = (f32[3,1,2,512]{3,2,1,0:T(2,128)S(1)}, f32[3,1,2,512]{3,2,1,0:T(2,128)S(1)}, u32[]{:S(2)}, u32[]{:S(2)}) collective-permute-start(f32[3,1,2,512]{3,2,1,0:T(2,128)S(1)} %get-tuple-element.103), channel_id=1, source_target_pairs={{1,0},{2,1},{3,2},{4,3},{5,4},{6,5},{7,6},{0,7},{9,8},{10,9},{11,1... | collective-permute-start | bytes 36872 | tf_op jit(solution)/shard_map/ppermute | solution.py:28
  76.6 1.3 %collective-permute-done.14 = f32[3,1,2,512]{3,2,1,0:T(2,128)S(1)} collective-permute-done((f32[3,1,2,512]{3,2,1,0:T(2,128)S(1)}, f32[3,1,2,512]{3,2,1,0:T(2,128)S(1)}, u32[]{:S(2)}, u32[]{:S(2)}) %collective-permute-start.14) | collective-permute-done | bytes 12320 | tf_op jit(solution)/shard_map/ppermute | solution.py:26
  78.8 3.6 %collective-permute-start.17 = (f32[3,1,2,512]{3,2,1,0:T(2,128)S(1)}, f32[3,1,2,512]{3,2,1,0:T(2,128)S(1)}, u32[]{:S(2)}, u32[]{:S(2)}) collective-permute-start(f32[3,1,2,512]{3,2,1,0:T(2,128)S(1)} %get-tuple-element.101), channel_id=1, source_target_pairs={{1,0},{2,1},{3,2},{4,3},{5,4},{6,5},{7,6},{0,7},{9,8},{10,9},{11,1... | collective-permute-start | bytes 36872 | tf_op jit(solution)/shard_map/ppermute | solution.py:28
  82.5 1.3 %collective-permute-done.16 = f32[3,1,2,512]{3,2,1,0:T(2,128)S(1)} collective-permute-done((f32[3,1,2,512]{3,2,1,0:T(2,128)S(1)}, f32[3,1,2,512]{3,2,1,0:T(2,128)S(1)}, u32[]{:S(2)}, u32[]{:S(2)}) %collective-permute-start.16) | collective-permute-done | bytes 12320 | tf_op jit(solution)/shard_map/ppermute | solution.py:26
  84.7 3.7 %collective-permute-start.19 = (f32[3,1,2,512]{3,2,1,0:T(2,128)S(1)}, f32[3,1,2,512]{3,2,1,0:T(2,128)S(1)}, u32[]{:S(2)}, u32[]{:S(2)}) collective-permute-start(f32[3,1,2,512]{3,2,1,0:T(2,128)S(1)} %get-tuple-element.99), channel_id=1, source_target_pairs={{1,0},{2,1},{3,2},{4,3},{5,4},{6,5},{7,6},{0,7},{9,8},{10,9},{11,1... | collective-permute-start | bytes 36872 | tf_op jit(solution)/shard_map/ppermute | solution.py:28
  88.6 1.1 collective-permute-done.18
  89.6 0.2 collective-permute-done.19
  90.3 1.4 %multiply_bitcast_fusion.2 = (f32[1,1,8,512]{3,2,1,0:T(8,128)S(1)}, f32[1,8,512]{2,1,0:T(8,128)S(1)}, f32[1,8,512]{2,1,0:T(8,128)}, f32[1,8,512]{2,1,0:T(8,128)S(1)}, f32[1,8,512]{2,1,0:T(8,128)}) fusion(f32[]{:T(128)} %bitcast.27, f32[1,8,512]{2,1,0:T(8,128)S(1)} %fusion.106, f32[1,8,512]{2,1,0:T(8,128)S(1)} %fusion.144, f32[1,8,512]{2,1,0:T(8,128)S(1)} %fusion.125, ...), kind=kLoop, calls=%fused_computation.359 | loop fusion | flops 200704 | bytes 393220 | tf_op jit(solution)/shard_map/stack | solution.py:129
  91.7 0.8 copy.509
  92.6 3.3 %reduce.2 = f32[512,3,8]{2,1,0:T(4,128)S(1)} reduce(f32[512,3,1,8]{3,2,1,0:T(1,128)S(1)} %bitcast.207, f32[]{:T(128)} %broadcast.650), dimensions={2}, to_apply=%bitcast.191.reduce_sub_computation | reduce | bytes 98308
  95.9 1.3 %reshape.1286 = f32[4,1,3072]{2,1,0:T(1,128)} reshape(f32[512,3,8]{2,1,0:T(4,128)S(1)} %reduce.2) | data formatting | bytes 98304
  97.2 3.3 %all-to-all-start.2 = ((f32[4,1,3072]{2,1,0:T(1,128)}), f32[4,1,3072]{2,1,0:T(1,128)S(1)}, u32[]{:S(2)}, u32[]{:S(2)}) async-start(f32[4,1,3072]{2,1,0:T(1,128)} %reshape.1286), calls=%async_computation.2 | async-start | bytes 98304 | tf_op jit(solution)/shard_map/all_to_all | solution.py:128
  100.6 2.0 %collective-permute-start.22 = (f32[12,4,10,1]{3,0,2,1:T(8,128)S(1)}, f32[12,4,10,1]{3,0,2,1:T(8,128)S(1)}, u32[]{:S(2)}, u32[]{:S(2)}) collective-permute-start(f32[12,4,10,1]{3,0,2,1:T(8,128)S(1)} %get-tuple-element.60), channel_id=1, source_target_pairs={{0,8},{8,16},{16,24},{24,0},{1,9},{9,17},{17,25},{25,1},{2,10},{10... | collective-permute-start | bytes 5768 | tf_op jit(solution)/shard_map/ppermute | solution.py:26
  102.6 1.0 collective-permute-start.23
  103.6 0.6 slice.1543
  104.2 1.1 all-to-all-done.2
  105.3 0.8 reduce.3
  106.1 1.3 %reshape.1287 = f32[512,3,1,8]{3,2,1,0:T(1,128)S(1)} reshape(f32[4,3072]{1,0:T(4,128)S(1)} %reduce.3) | data formatting | bytes 98304
  107.3 0.9 copy.510
  108.3 3.3 %collective-permute-done.22 = f32[12,4,10,1]{3,0,2,1:T(8,128)S(1)} collective-permute-done((f32[12,4,10,1]{3,0,2,1:T(8,128)S(1)}, f32[12,4,10,1]{3,0,2,1:T(8,128)S(1)}, u32[]{:S(2)}, u32[]{:S(2)}) %collective-permute-start.22) | collective-permute-done | bytes 1952 | tf_op jit(solution)/shard_map/ppermute | solution.py:26
  111.6 3.6 %collective-permute-done.23 = f32[12,4,10,1]{3,0,2,1:T(8,128)S(1)} collective-permute-done((f32[12,4,10,1]{3,0,2,1:T(8,128)S(1)}, f32[12,4,10,1]{3,0,2,1:T(8,128)S(1)}, u32[]{:S(2)}, u32[]{:S(2)}) %collective-permute-start.23) | collective-permute-done | bytes 1952 | tf_op jit(solution)/shard_map/ppermute | solution.py:28
  115.1 0.4 fusion.10
  115.6 0.4 fusion.1
  116.0 0.7 copy.512
  (171 shorter events, 7.9 us)
Async XLA Ops:
  0.6 54.0 %copy-start = (f32[12,12]{1,0:T(8,128)S(1)}, f32[12,12]{1,0:T(8,128)}, u32[]{:S(2)}) copy-start(f32[12,12]{1,0:T(8,128)} %param.17) | copy-start | bytes 1732
  1.5 13.0 %collective-permute-start = (f32[3,1,2,512]{3,2,1,0:T(2,128)S(1)}, f32[3,1,2,512]{3,2,1,0:T(2,128)S(1)}, u32[]{:S(2)}, u32[]{:S(2)}) collective-permute-start(f32[3,1,2,512]{3,2,1,0:T(2,128)S(1)} %get-tuple-element.118), channel_id=1, source_target_pairs={{0,1},{1,2},{2,3},{3,4},{4,5},{5,6},{6,7},{7,0},{8,9},{9,10},{10,1... | collective-permute-start | bytes 36872 | tf_op jit(solution)/shard_map/ppermute | solution.py:26
  2.0 12.4 %collective-permute-start.1 = (f32[3,1,2,512]{3,2,1,0:T(2,128)S(1)}, f32[3,1,2,512]{3,2,1,0:T(2,128)S(1)}, u32[]{:S(2)}, u32[]{:S(2)}) collective-permute-start(f32[3,1,2,512]{3,2,1,0:T(2,128)S(1)} %get-tuple-element.119), channel_id=1, source_target_pairs={{1,0},{2,1},{3,2},{4,3},{5,4},{6,5},{7,6},{0,7},{9,8},{10,9},{11,1... | collective-permute-start | bytes 36872 | tf_op jit(solution)/shard_map/ppermute | solution.py:28
  7.1 3.6 %copy-start.3 = (f32[1,8,512]{2,1,0:T(8,128)S(1)}, f32[1,8,512]{2,1,0:T(8,128)}, u32[]{:S(2)}) copy-start(f32[1,8,512]{2,1,0:T(8,128)} %param.10) | copy-start | bytes 49156
  7.2 17.6 %collective-permute-start.8 = (f32[12,4,1,128]{3,0,2,1:T(8,128)S(1)}, f32[12,4,1,128]{3,0,2,1:T(8,128)S(1)}, u32[]{:S(2)}, u32[]{:S(2)}) collective-permute-start(f32[12,4,1,128]{3,0,2,1:T(8,128)S(1)} %get-tuple-element.66), channel_id=1, source_target_pairs={{0,1},{1,2},{2,3},{3,4},{4,5},{5,6},{6,7},{7,0},{8,9},{9,10},{10,1... | collective-permute-start | bytes 73736 | tf_op jit(solution)/shard_map/ppermute | solution.py:26
  7.2 17.7 %collective-permute-start.9 = (f32[12,4,1,128]{3,0,2,1:T(8,128)S(1)}, f32[12,4,1,128]{3,0,2,1:T(8,128)S(1)}, u32[]{:S(2)}, u32[]{:S(2)}) collective-permute-start(f32[12,4,1,128]{3,0,2,1:T(8,128)S(1)} %get-tuple-element.67), channel_id=1, source_target_pairs={{1,0},{2,1},{3,2},{4,3},{5,4},{6,5},{7,6},{0,7},{9,8},{10,9},{11,1... | collective-permute-start | bytes 73736 | tf_op jit(solution)/shard_map/ppermute | solution.py:28
  10.8 0.7 copy-start.4
  11.6 0.7 copy-start.1
  12.4 0.7 copy-start.8
  13.1 1.4 %copy-start.7 = (f32[1,8,512]{2,1,0:T(8,128)S(1)}, f32[1,8,512]{2,1,0:T(8,128)}, u32[]{:S(2)}) copy-start(f32[1,8,512]{2,1,0:T(8,128)} %param.12) | copy-start | bytes 49156
  13.1 0.7 copy-start.11
  15.3 5.0 %collective-permute-start.2 = (f32[3,1,2,512]{3,2,1,0:T(2,128)S(1)}, f32[3,1,2,512]{3,2,1,0:T(2,128)S(1)}, u32[]{:S(2)}, u32[]{:S(2)}) collective-permute-start(f32[3,1,2,512]{3,2,1,0:T(2,128)S(1)} %get-tuple-element.116), channel_id=1, source_target_pairs={{0,1},{1,2},{2,3},{3,4},{4,5},{5,6},{6,7},{7,0},{8,9},{9,10},{10,1... | collective-permute-start | bytes 36872 | tf_op jit(solution)/shard_map/ppermute | solution.py:26
  15.4 4.9 %collective-permute-start.3 = (f32[3,1,2,512]{3,2,1,0:T(2,128)S(1)}, f32[3,1,2,512]{3,2,1,0:T(2,128)S(1)}, u32[]{:S(2)}, u32[]{:S(2)}) collective-permute-start(f32[3,1,2,512]{3,2,1,0:T(2,128)S(1)} %get-tuple-element.117), channel_id=1, source_target_pairs={{1,0},{2,1},{3,2},{4,3},{5,4},{6,5},{7,6},{0,7},{9,8},{10,9},{11,1... | collective-permute-start | bytes 36872 | tf_op jit(solution)/shard_map/ppermute | solution.py:28
  21.0 3.8 %copy-start.2 = (f32[12,4,8,128]{3,2,1,0:T(8,128)S(1)}, f32[12,4,8,128]{3,2,1,0:T(8,128)}, u32[]{:S(2)}) copy-start(f32[12,4,8,128]{3,2,1,0:T(8,128)} %param.16) | copy-start | bytes 589828
  21.2 8.3 %collective-permute-start.4 = (f32[3,1,2,512]{3,2,1,0:T(2,128)S(1)}, f32[3,1,2,512]{3,2,1,0:T(2,128)S(1)}, u32[]{:S(2)}, u32[]{:S(2)}) collective-permute-start(f32[3,1,2,512]{3,2,1,0:T(2,128)S(1)} %get-tuple-element.114), channel_id=1, source_target_pairs={{0,1},{1,2},{2,3},{3,4},{4,5},{5,6},{6,7},{7,0},{8,9},{9,10},{10,1... | collective-permute-start | bytes 36872 | tf_op jit(solution)/shard_map/ppermute | solution.py:26
  21.2 8.2 %collective-permute-start.5 = (f32[3,1,2,512]{3,2,1,0:T(2,128)S(1)}, f32[3,1,2,512]{3,2,1,0:T(2,128)S(1)}, u32[]{:S(2)}, u32[]{:S(2)}) collective-permute-start(f32[3,1,2,512]{3,2,1,0:T(2,128)S(1)} %get-tuple-element.115), channel_id=1, source_target_pairs={{1,0},{2,1},{3,2},{4,3},{5,4},{6,5},{7,6},{0,7},{9,8},{10,9},{11,1... | collective-permute-start | bytes 36872 | tf_op jit(solution)/shard_map/ppermute | solution.py:28
  24.9 0.6 copy-start.5
  26.5 26.9 %collective-permute-start.10 = (f32[12,4,10,1]{3,0,2,1:T(8,128)}, f32[12,4,10,1]{3,0,2,1:T(8,128)S(1)}, u32[]{:S(2)}, u32[]{:S(2)}) collective-permute-start(f32[12,4,10,1]{3,0,2,1:T(8,128)} %get-tuple-element.62), channel_id=1, source_target_pairs={{0,8},{8,16},{16,24},{24,0},{1,9},{9,17},{17,25},{25,1},{2,10},{10... | collective-permute-start | bytes 5768 | tf_op jit(solution)/shard_map/ppermute | solution.py:26
  28.5 25.0 %collective-permute-start.11 = (f32[12,4,10,1]{3,0,2,1:T(8,128)S(1)}, f32[12,4,10,1]{3,0,2,1:T(8,128)S(1)}, u32[]{:S(2)}, u32[]{:S(2)}) collective-permute-start(f32[12,4,10,1]{3,0,2,1:T(8,128)S(1)} %get-tuple-element.63), channel_id=1, source_target_pairs={{8,0},{16,8},{24,16},{0,24},{9,1},{17,9},{25,17},{1,25},{10,2},{18... | collective-permute-start | bytes 5768 | tf_op jit(solution)/shard_map/ppermute | solution.py:28
  30.2 5.0 %collective-permute-start.6 = (f32[3,1,2,512]{3,2,1,0:T(2,128)S(1)}, f32[3,1,2,512]{3,2,1,0:T(2,128)S(1)}, u32[]{:S(2)}, u32[]{:S(2)}) collective-permute-start(f32[3,1,2,512]{3,2,1,0:T(2,128)S(1)} %get-tuple-element.112), channel_id=1, source_target_pairs={{0,1},{1,2},{2,3},{3,4},{4,5},{5,6},{6,7},{7,0},{8,9},{9,10},{10,1... | collective-permute-start | bytes 36872 | tf_op jit(solution)/shard_map/ppermute | solution.py:26
  30.2 4.9 %collective-permute-start.7 = (f32[3,1,2,512]{3,2,1,0:T(2,128)S(1)}, f32[3,1,2,512]{3,2,1,0:T(2,128)S(1)}, u32[]{:S(2)}, u32[]{:S(2)}) collective-permute-start(f32[3,1,2,512]{3,2,1,0:T(2,128)S(1)} %get-tuple-element.113), channel_id=1, source_target_pairs={{1,0},{2,1},{3,2},{4,3},{5,4},{6,5},{7,6},{0,7},{9,8},{10,9},{11,1... | collective-permute-start | bytes 36872 | tf_op jit(solution)/shard_map/ppermute | solution.py:28
  42.4 8.1 %all-to-all-start = ((f32[4,1,3072]{2,1,0:T(1,128)}), f32[4,1,3072]{2,1,0:T(1,128)S(1)}, u32[]{:S(2)}, u32[]{:S(2)}) async-start(f32[4,1,3072]{2,1,0:T(1,128)} %reshape.1284), calls=%async_computation | async-start | bytes 98304 | tf_op jit(solution)/shard_map/all_to_all | solution.py:128
  53.4 0.8 copy-start.6
  54.6 0.7 copy-start.9
  55.6 0.7 copy-start.10
  56.9 7.9 %all-to-all-start.1 = ((f32[4,8,128]{2,1,0:T(8,128)}), f32[4,8,128]{2,1,0:T(8,128)S(1)}, u32[]{:S(2)}, u32[]{:S(2)}) async-start(f32[4,8,128]{2,1,0:T(8,128)} %broadcast_multiply_fusion), calls=%async_computation.1 | async-start | bytes 32768 | tf_op jit(solution)/shard_map/all_to_all | solution.py:154
  64.8 7.2 %collective-permute-start.12 = (f32[3,1,2,512]{3,2,1,0:T(2,128)S(1)}, f32[3,1,2,512]{3,2,1,0:T(2,128)S(1)}, u32[]{:S(2)}, u32[]{:S(2)}) collective-permute-start(f32[3,1,2,512]{3,2,1,0:T(2,128)S(1)} %get-tuple-element.104), channel_id=1, source_target_pairs={{0,1},{1,2},{2,3},{3,4},{4,5},{5,6},{6,7},{7,0},{8,9},{9,10},{10,1... | collective-permute-start | bytes 36872 | tf_op jit(solution)/shard_map/ppermute | solution.py:26
  64.9 7.1 %collective-permute-start.13 = (f32[3,1,2,512]{3,2,1,0:T(2,128)S(1)}, f32[3,1,2,512]{3,2,1,0:T(2,128)S(1)}, u32[]{:S(2)}, u32[]{:S(2)}) collective-permute-start(f32[3,1,2,512]{3,2,1,0:T(2,128)S(1)} %get-tuple-element.105), channel_id=1, source_target_pairs={{1,0},{2,1},{3,2},{4,3},{5,4},{6,5},{7,6},{0,7},{9,8},{10,9},{11,1... | collective-permute-start | bytes 36872 | tf_op jit(solution)/shard_map/ppermute | solution.py:28
  68.5 8.1 %collective-permute-start.20 = (f32[12,4,1,128]{3,0,2,1:T(8,128)S(1)}, f32[12,4,1,128]{3,0,2,1:T(8,128)S(1)}, u32[]{:S(2)}, u32[]{:S(2)}) collective-permute-start(f32[12,4,1,128]{3,0,2,1:T(8,128)S(1)} %get-tuple-element.64), channel_id=1, source_target_pairs={{0,1},{1,2},{2,3},{3,4},{4,5},{5,6},{6,7},{7,0},{8,9},{9,10},{10,1... | collective-permute-start | bytes 73736 | tf_op jit(solution)/shard_map/ppermute | solution.py:26
  68.5 8.1 %collective-permute-start.21 = (f32[12,4,1,128]{3,0,2,1:T(8,128)S(1)}, f32[12,4,1,128]{3,0,2,1:T(8,128)S(1)}, u32[]{:S(2)}, u32[]{:S(2)}) collective-permute-start(f32[12,4,1,128]{3,0,2,1:T(8,128)S(1)} %get-tuple-element.65), channel_id=1, source_target_pairs={{1,0},{2,1},{3,2},{4,3},{5,4},{6,5},{7,6},{0,7},{9,8},{10,9},{11,1... | collective-permute-start | bytes 73736 | tf_op jit(solution)/shard_map/ppermute | solution.py:28
  72.9 5.0 %collective-permute-start.14 = (f32[3,1,2,512]{3,2,1,0:T(2,128)S(1)}, f32[3,1,2,512]{3,2,1,0:T(2,128)S(1)}, u32[]{:S(2)}, u32[]{:S(2)}) collective-permute-start(f32[3,1,2,512]{3,2,1,0:T(2,128)S(1)} %get-tuple-element.102), channel_id=1, source_target_pairs={{0,1},{1,2},{2,3},{3,4},{4,5},{5,6},{6,7},{7,0},{8,9},{9,10},{10,1... | collective-permute-start | bytes 36872 | tf_op jit(solution)/shard_map/ppermute | solution.py:26
  73.0 4.9 %collective-permute-start.15 = (f32[3,1,2,512]{3,2,1,0:T(2,128)S(1)}, f32[3,1,2,512]{3,2,1,0:T(2,128)S(1)}, u32[]{:S(2)}, u32[]{:S(2)}) collective-permute-start(f32[3,1,2,512]{3,2,1,0:T(2,128)S(1)} %get-tuple-element.103), channel_id=1, source_target_pairs={{1,0},{2,1},{3,2},{4,3},{5,4},{6,5},{7,6},{0,7},{9,8},{10,9},{11,1... | collective-permute-start | bytes 36872 | tf_op jit(solution)/shard_map/ppermute | solution.py:28
  78.8 5.0 %collective-permute-start.16 = (f32[3,1,2,512]{3,2,1,0:T(2,128)S(1)}, f32[3,1,2,512]{3,2,1,0:T(2,128)S(1)}, u32[]{:S(2)}, u32[]{:S(2)}) collective-permute-start(f32[3,1,2,512]{3,2,1,0:T(2,128)S(1)} %get-tuple-element.100), channel_id=1, source_target_pairs={{0,1},{1,2},{2,3},{3,4},{4,5},{5,6},{6,7},{7,0},{8,9},{9,10},{10,1... | collective-permute-start | bytes 36872 | tf_op jit(solution)/shard_map/ppermute | solution.py:26
  78.8 5.0 %collective-permute-start.17 = (f32[3,1,2,512]{3,2,1,0:T(2,128)S(1)}, f32[3,1,2,512]{3,2,1,0:T(2,128)S(1)}, u32[]{:S(2)}, u32[]{:S(2)}) collective-permute-start(f32[3,1,2,512]{3,2,1,0:T(2,128)S(1)} %get-tuple-element.101), channel_id=1, source_target_pairs={{1,0},{2,1},{3,2},{4,3},{5,4},{6,5},{7,6},{0,7},{9,8},{10,9},{11,1... | collective-permute-start | bytes 36872 | tf_op jit(solution)/shard_map/ppermute | solution.py:28
  84.7 5.0 %collective-permute-start.18 = (f32[3,1,2,512]{3,2,1,0:T(2,128)S(1)}, f32[3,1,2,512]{3,2,1,0:T(2,128)S(1)}, u32[]{:S(2)}, u32[]{:S(2)}) collective-permute-start(f32[3,1,2,512]{3,2,1,0:T(2,128)S(1)} %get-tuple-element.98), channel_id=1, source_target_pairs={{0,1},{1,2},{2,3},{3,4},{4,5},{5,6},{6,7},{7,0},{8,9},{9,10},{10,1... | collective-permute-start | bytes 36872 | tf_op jit(solution)/shard_map/ppermute | solution.py:26
  84.7 5.2 %collective-permute-start.19 = (f32[3,1,2,512]{3,2,1,0:T(2,128)S(1)}, f32[3,1,2,512]{3,2,1,0:T(2,128)S(1)}, u32[]{:S(2)}, u32[]{:S(2)}) collective-permute-start(f32[3,1,2,512]{3,2,1,0:T(2,128)S(1)} %get-tuple-element.99), channel_id=1, source_target_pairs={{1,0},{2,1},{3,2},{4,3},{5,4},{6,5},{7,6},{0,7},{9,8},{10,9},{11,1... | collective-permute-start | bytes 36872 | tf_op jit(solution)/shard_map/ppermute | solution.py:28
  97.2 8.2 %all-to-all-start.2 = ((f32[4,1,3072]{2,1,0:T(1,128)}), f32[4,1,3072]{2,1,0:T(1,128)S(1)}, u32[]{:S(2)}, u32[]{:S(2)}) async-start(f32[4,1,3072]{2,1,0:T(1,128)} %reshape.1286), calls=%async_computation.2 | async-start | bytes 98304 | tf_op jit(solution)/shard_map/all_to_all | solution.py:128
  100.6 11.0 %collective-permute-start.22 = (f32[12,4,10,1]{3,0,2,1:T(8,128)S(1)}, f32[12,4,10,1]{3,0,2,1:T(8,128)S(1)}, u32[]{:S(2)}, u32[]{:S(2)}) collective-permute-start(f32[12,4,10,1]{3,0,2,1:T(8,128)S(1)} %get-tuple-element.60), channel_id=1, source_target_pairs={{0,8},{8,16},{16,24},{24,0},{1,9},{9,17},{17,25},{25,1},{2,10},{10... | collective-permute-start | bytes 5768 | tf_op jit(solution)/shard_map/ppermute | solution.py:26
  102.6 12.5 %collective-permute-start.23 = (f32[12,4,10,1]{3,0,2,1:T(8,128)S(1)}, f32[12,4,10,1]{3,0,2,1:T(8,128)S(1)}, u32[]{:S(2)}, u32[]{:S(2)}) collective-permute-start(f32[12,4,10,1]{3,0,2,1:T(8,128)S(1)} %get-tuple-element.61), channel_id=1, source_target_pairs={{8,0},{16,8},{24,16},{0,24},{9,1},{17,9},{25,17},{1,25},{10,2},{18... | collective-permute-start | bytes 5768 | tf_op jit(solution)/shard_map/ppermute | solution.py:28
where the time goes:
time: 118 us; the launch traced here: 117 us
  starting transfers between devices  52.9 us (45%)
  waiting for transfers between devices  23.8 us (20%)
  local copies, waits for them, and re-layouts  22.7 us (19%)
  other arithmetic  14.9 us (13%)
  between operations  1.32 us (1%)
    ppermute x12, starting transfers between devices, padded_2(): lax.ppermute(head, axis, [((i + 1) % count, i) for i in range(count)])  38.1 us
    unnamed x33, local copies, waits for them, and re-layouts  12.3 us
    ppermute x12, waiting for transfers between devices, padded_2(): lax.ppermute(tail, axis, [(i, (i + 1) % count) for i in range(count)])  9.59 us
    unnamed x2, other arithmetic  6.67 us
    all_to_all x2, starting transfers between devices, body(): lax.all_to_all(jnp.stack([zonal_mean, merid_mean, kappa_rows]), 'sect', s...  6.55 us
    all_to_all x2, waiting for transfers between devices, body(): lax.all_to_all(jnp.stack([zonal_mean, merid_mean, kappa_rows]), 'sect', s...  5.67 us
    ppermute x12, starting transfers between devices, padded_2(): lax.ppermute(tail, axis, [(i, (i + 1) % count) for i in range(count)])  4.97 us
    all_to_all x1, waiting for transfers between devices, body(): lax.all_to_all(heat_cols, 'sect', split_axis=0, concat_axis=2, tiled=True)  4.61 us
  transfers between devices with their start and end apart: 27, of which 12 were waited for; matrix products, arithmetic and copies ran while one was open for 18% of the time, Pallas kernels for 0%

commit v1 on v0

v1 whole, which is shorter than its diff:
```python
import functools

import jax
import jax.numpy as jnp
from jax import lax
from jax.experimental import pallas as pl
from jax.experimental.pallas import tpu as pltpu
from jax.sharding import PartitionSpec as P

STEPS = 4
INTERVALS = 2

time_step = 0.1
gravity = 1.0
coriolis = 0.3
viscosity = 0.05
heat_coupling = 0.05
tracer_step = 0.5
stir_gain = 4.0

LANES = 128


def ocean_steps(zonal, merid, height, wet, forcing, rows):
    tall, wide = zonal.shape

    def east(a):
        return pltpu.roll(a, wide - 1, 1)

    def west(a):
        return pltpu.roll(a, 1, 1)

    def north(a):
        return pltpu.roll(a, tall - 1, 0)

    def south(a):
        return pltpu.roll(a, 1, 0)

    own = slice(rows, 2 * rows)
    zonal_sum = jnp.zeros((rows, wide), jnp.float32)
    merid_sum = jnp.zeros((rows, wide), jnp.float32)
    for _ in range(STEPS):
        ze, zw, zn, zs = east(zonal), west(zonal), north(zonal), south(zonal)
        me, mw, mn, ms = east(merid), west(merid), north(merid), south(merid)
        height = height - (0.5 * time_step) * ((ze - zw) + (mn - ms))
        if forcing is not None:
            height = height + (time_step * heat_coupling) * forcing
        zonal_lap = zn + zs + ze + zw - 4.0 * zonal
        merid_lap = mn + ms + me + mw - 4.0 * merid
        zonal_new = wet * (
            zonal
            + time_step
            * (
                coriolis * merid
                - (0.5 * gravity) * (east(height) - west(height))
                + viscosity * zonal_lap
            )
        )
        merid_new = wet * (
            merid
            + time_step
            * (
                -coriolis * zonal
                - (0.5 * gravity) * (north(height) - south(height))
                + viscosity * merid_lap
            )
        )
        zonal, merid = zonal_new, merid_new
        zonal_sum = zonal_sum + zonal[own]
        merid_sum = merid_sum + merid[own]
    return zonal[own], merid[own], height[own], zonal_sum / STEPS, merid_sum / STEPS


def kernel(
    sects,
    tiles,
    zonal_in,
    merid_in,
    height_in,
    sea_in,
    flags_in,
    conc_in,
    kappa_in,
    react_in,
    absorb_in,
    light_in,
    conc_out,
    zonal_out,
    merid_out,
    height_out,
    ocean,
    sea,
    flags,
    conc,
    react_d,
    base,
    west_v,
    east_v,
    south_v,
    north_v,
    cols_send,
    cols_recv,
    rows_send,
    rows_recv,
    state_send,
    mean_send,
    mean_recv,
    heat_send,
    heat_recv,
    local_sem,
    first_send,
    first_recv,
    state_ssem,
    state_rsem,
    halo_ssem,
    halo_rsem,
    mean_ssem,
    mean_rsem,
    heat_ssem,
    heat_rsem,
):
    me_s = lax.axis_index("sect")
    me_t = lax.axis_index("tile")
    tracers, levels, rows, columns = conc_in.shape
    depth = zonal_in.shape[0]
    above = lax.rem(me_t + 1, tiles)
    below = lax.rem(me_t + tiles - 1, tiles)
    steps_t = {1: above, 0: me_t, -1: below}

    def sect_at(offset):
        return lax.rem(me_s + offset, sects)

    def remote(src, dst, send, recv, to_s, to_t):
        return pltpu.make_async_remote_copy(
            src_ref=src,
            dst_ref=dst,
            send_sem=send,
            recv_sem=recv,
            device_id=(to_s, to_t),
            device_id_type=pl.DeviceIdType.MESH,
        )

    def slot(step):
        return pl.ds((1 - step) * rows, rows)

    fields_in = (zonal_in, merid_in, height_in)
    local = [
        pltpu.make_async_copy(conc_in, conc, local_sem.at[0]),
        pltpu.make_async_copy(flags_in, flags, local_sem.at[1]),
        pltpu.make_async_copy(sea_in, sea.at[slot(0)], local_sem.at[2]),
    ] + [
        pltpu.make_async_copy(field, ocean.at[0, f, :, slot(0)], local_sem.at[3 + f])
        for f, field in enumerate(fields_in)
    ]
    barrier = pltpu.get_barrier_semaphore()
    peers = [(o, d) for o in range(sects) for d in (1, -1, 0) if (o, d) != (0, 0)]
    for o, d in peers:
        pl.semaphore_signal(
            barrier,
            inc=1,
            device_id=(sect_at(o), steps_t[d]),
            device_id_type=pl.DeviceIdType.MESH,
        )
    for copy in local:
        copy.start()
    pl.semaphore_wait(barrier, len(peers))

    first = []
    for i, d in enumerate((1, -1)):
        for f, field in enumerate(fields_in):
            first.append(
                remote(
                    field,
                    ocean.at[0, f, :, slot(d)],
                    first_send.at[i, f],
                    first_recv.at[i, f],
                    me_s,
                    steps_t[d],
                )
            )
        first.append(
            remote(
                sea_in,
                sea.at[slot(d)],
                first_send.at[i, 3],
                first_recv.at[i, 3],
                me_s,
                steps_t[d],
            )
        )
    for copy in first:
        copy.start()
    sent = list(first)

    lane = lax.broadcasted_iota(jnp.int32, (rows, columns), 1)
    row = lax.broadcasted_iota(jnp.int32, (rows, columns), 0)

    for copy in local[:3]:
        copy.wait()
    own_columns = pl.ds(pl.multiple_of(me_s * columns, LANES), columns)
    sea_cols = sea[slot(0), own_columns]
    wet_cols = sea_cols.astype(jnp.float32)
    is_wet = sea_cols == 1

    def react_and_send(turn, heated):
        names = tracers + (1 if heated else 0)
        cells = names * levels
        to_east = [jnp.zeros((rows, columns), jnp.float32) for _ in range(pl.cdiv(cells, LANES))]
        to_west = list(to_east)
        for k in range(levels):
            old = [conc[i, k] for i in range(tracers)]
            heat_d = None
            for i in range(names):
                n = i * levels + k
                if i < tracers:
                    growth = react_in[i, 0] * old[0]
                    for j in range(1, tracers):
                        growth = growth + react_in[i, j] * old[j]
                    new = old[i] + tracer_step * growth
                    kept = jnp.where(is_wet, new, old[i])
                    if heated:
                        a = absorb_in[i]
                        heat_d = a * new if i == 0 else heat_d + a * new
                        heat_b = a * kept if i == 0 else heat_b + a * kept
                else:
                    new, kept = heat_d, heat_b
                react_d[n] = new
                base[n] = kept
                rows_send[turn, 0, pl.ds(n, 1)] = new[rows - 1 : rows]
                rows_send[turn, 1, pl.ds(n, 1)] = new[0:1]
                p, at = divmod(n, LANES)
                here = lane == at
                turned = pltpu.roll(new, (at + 1) % columns, 1)
                to_east[p] = jnp.where(here, turned, to_east[p])
                turned = pltpu.roll(new, at, 1) if at else new
                to_west[p] = jnp.where(here, turned, to_west[p])
        for p in range(len(to_east)):
            cols_send[turn, 0, p] = to_east[p]
            cols_send[turn, 1, p] = to_west[p]
        copies = []
        for i, d in enumerate((1, -1)):
            copies.append(
                remote(
                    rows_send.at[turn, i],
                    rows_recv.at[turn, i],
                    halo_ssem.at[turn, i],
                    halo_rsem.at[turn, i],
                    me_s,
                    steps_t[d],
                )
            )
            copies.append(
                remote(
                    cols_send.at[turn, i],
                    cols_recv.at[turn, i],
                    halo_ssem.at[turn, 2 + i],
                    halo_rsem.at[turn, 2 + i],
                    sect_at(1 if i == 0 else sects - 1),
                    me_t,
                )
            )
        for copy in copies:
            copy.start()
        sent.extend(copies)
        return copies, cells

    def shift_cells(turn, cells):
        from_west = [cols_recv[turn, 0, p] for p in range(pl.cdiv(cells, LANES))]
        from_east = [cols_recv[turn, 1, p] for p in range(pl.cdiv(cells, LANES))]
        for n in range(cells):
            p, at = divmod(n, LANES)
            new = react_d[n]
            edge = pltpu.roll(from_west[p], columns - at, 1) if at else from_west[p]
            west_v[n] = jnp.where(lane == 0, edge, pltpu.roll(new, 1, 1))
            edge = pltpu.roll(from_east[p], columns - 1 - at, 1) if at < columns - 1 else from_east[p]
            east_v[n] = jnp.where(lane == columns - 1, edge, pltpu.roll(new, columns - 1, 1))
            edge = jnp.broadcast_to(rows_recv[turn, 0, pl.ds(n, 1)], (rows, columns))
            south_v[n] = jnp.where(row == 0, edge, pltpu.roll(new, 1, 0))
            edge = jnp.broadcast_to(rows_recv[turn, 1, pl.ds(n, 1)], (rows, columns))
            north_v[n] = jnp.where(row == rows - 1, edge, pltpu.roll(new, rows - 1, 0))

    def send_means(turn, means):
        copies = []
        for l, pair in enumerate(means):
            for f, mean in enumerate(pair):
                for s in range(sects):
                    mean_send[turn, s, f, l] = mean[:, s * columns : (s + 1) * columns]
        for o in range(1, sects):
            to = sect_at(o)
            copies.append(
                remote(
                    mean_send.at[turn, to],
                    mean_recv.at[turn, me_s],
                    mean_ssem.at[turn, o],
                    mean_rsem.at[turn, o],
                    to,
                    me_t,
                )
            )
        for copy in copies:
            copy.start()
        sent.extend(copies)
        mean_recv[turn, me_s] = mean_send[turn, me_s]
        return copies

    def column_terms(turn):
        kappa, stencil = [], []
        half_wet = tracer_step * wet_cols
        for k in range(levels):
            along_x = mean_recv[turn, k // depth, 0, k % depth]
            along_y = mean_recv[turn, k // depth, 1, k % depth]
            kappa.append(kappa_in[k] * (1.0 + stir_gain * (along_x * along_x + along_y * along_y)))
            upwind = flags[k] == 1
            terms = []
            for speed in (along_x, along_y):
                terms.append(half_wet * jnp.where(upwind, jnp.maximum(speed, 0.0), 0.5 * speed))
                terms.append(half_wet * jnp.where(upwind, jnp.minimum(speed, 0.0), 0.5 * speed))
            stencil.append(terms)
        couple = [tracer_step * 0.5 * (kappa[k] + kappa[k + 1]) for k in range(levels - 1)]
        out, factor = [], None
        for k in range(levels):
            denom = 1.0
            if k > 0:
                denom = denom + couple[k - 1]
            if k < levels - 1:
                denom = denom + couple[k]
            if k > 0:
                denom = denom + couple[k - 1] * factor
            inverse = 1.0 / denom
            px, qx, py, qy = stencil[k]
            out.append(
                dict(
                    centre=inverse * (1.0 - ((px - qx) + (py - qy))),
                    west=inverse * px,
                    east=inverse * qx,
                    south=inverse * py,
                    north=inverse * qy,
                    lower=inverse * couple[k - 1] if k > 0 else None,
                    upper=inverse * couple[k] if k < levels - 1 else None,
                )
            )
            factor = -out[k]["upper"] if k < levels - 1 else None
        return out

    def tracer_column(terms, i):
        partial = []
        for k in range(levels):
            n = i * levels + k
            t = terms[k]
            now = (
                t["centre"] * base[n]
                + (t["west"] * west_v[n] - t["east"] * east_v[n])
                + (t["south"] * south_v[n] - t["north"] * north_v[n])
            )
            if k > 0:
                now = now + t["lower"] * partial[k - 1]
            partial.append(now)
        for k in range(levels - 2, -1, -1):
            partial[k] = partial[k] + terms[k]["upper"] * partial[k + 1]
        return partial

    halo0, cells0 = react_and_send(0, True)
    for copy in local[3:]:
        copy.wait()
    for copy in first:
        copy.wait_recv()
    wet = sea[...].astype(jnp.float32)
    means = []
    for l in range(depth):
        z, m, h, zm, mm = ocean_steps(
            ocean[0, 0, l], ocean[0, 1, l], ocean[0, 2, l], wet, None, rows
        )
        means.append((zm, mm))
        for f, value in enumerate((z, m, h)):
            state_send[f, l] = value
    got = send_means(0, means)
    state = []
    for i, d in enumerate((1, -1)):
        state.append(
            remote(
                state_send,
                ocean.at[1, :, :, slot(d)],
                state_ssem.at[i],
                state_rsem.at[i],
                me_s,
                steps_t[d],
            )
        )
    for copy in state:
        copy.start()
    sent.extend(state)
    for f in range(3):
        for l in range(depth):
            ocean[1, f, l, slot(0)] = state_send[f, l]
    for copy in halo0:
        copy.wait_recv()
    shift_cells(0, cells0)
    for copy in got:
        copy.wait_recv()
    terms = column_terms(0)

    heat = tracer_column(terms, tracers)
    for k in range(levels):
        heat_send[k // depth, k % depth] = light_in[k] * heat[k]
    heats = []
    for o in range(sects - 1, -1, -1):
        for i, d in enumerate((1, -1, 0)):
            if (o, d) == (0, 0):
                continue
            to = sect_at(o)
            heats.append(
                remote(
                    heat_send.at[to],
                    heat_recv.at[me_s, :, slot(d)],
                    heat_ssem.at[o, i],
                    heat_rsem.at[o, i],
                    to,
                    steps_t[d],
                )
            )
    for copy in heats:
        copy.start()
    sent.extend(heats)
    heat_recv[me_s, :, slot(0)] = heat_send[me_s]

    for i in range(tracers):
        for k, value in enumerate(tracer_column(terms, i)):
            conc[i, k] = value
    halo1, cells1 = react_and_send(1, False)
    for copy in halo1:
        copy.wait_recv()
    shift_cells(1, cells1)

    for copy in state:
        copy.wait_recv()
    for copy in heats:
        copy.wait_recv()
    means = []
    for l in range(depth):
        forcing = jnp.concatenate([heat_recv[s, l] for s in range(sects)], axis=1)
        z, m, h, zm, mm = ocean_steps(
            ocean[1, 0, l], ocean[1, 1, l], ocean[1, 2, l], wet, forcing, rows
        )
        means.append((zm, mm))
        zonal_out[l] = z
        merid_out[l] = m
        height_out[l] = h
    got = send_means(1, means)
    for copy in got:
        copy.wait_recv()
    terms = column_terms(1)
    for i in range(tracers):
        for k, value in enumerate(tracer_column(terms, i)):
            conc_out[i, k] = value
    for copy in sent:
        copy.wait_send()


def body(sects, tiles, zonal, merid, height, level_kappa, sea, flags, conc, react, absorb, light):
    tracers, levels, rows, columns = conc.shape
    depth, _, wide = zonal.shape
    assert rows >= 2 * STEPS and columns % LANES == 0 and INTERVALS == 2
    cells = (tracers + 1) * levels
    packs = pl.cdiv(cells, LANES)
    padded = pl.cdiv(cells, 8) * 8
    f32 = jnp.float32
    dma = pltpu.SemaphoreType.DMA
    any_space = pl.BlockSpec(memory_space=pl.ANY)
    smem = pl.BlockSpec(memory_space=pltpu.SMEM)
    vmem = pl.BlockSpec(memory_space=pltpu.VMEM)
    return pl.pallas_call(
        functools.partial(kernel, sects, tiles),
        out_shape=[
            jax.ShapeDtypeStruct(conc.shape, f32),
            jax.ShapeDtypeStruct(zonal.shape, f32),
            jax.ShapeDtypeStruct(merid.shape, f32),
            jax.ShapeDtypeStruct(height.shape, f32),
        ],
        in_specs=[any_space] * 6 + [smem] * 4,
        out_specs=[vmem] * 4,
        scratch_shapes=[
            pltpu.VMEM((2, 3, depth, 3 * rows, wide), f32),
            pltpu.VMEM((3 * rows, wide), jnp.int32),
            pltpu.VMEM(flags.shape, jnp.int32),
            pltpu.VMEM(conc.shape, f32),
        ]
        + [pltpu.VMEM((cells, rows, columns), f32)] * 6
        + [
            pltpu.VMEM((2, 2, packs, rows, columns), f32),
            pltpu.VMEM((2, 2, packs, rows, columns), f32),
            pltpu.VMEM((2, 2, padded, columns), f32),
            pltpu.VMEM((2, 2, padded, columns), f32),
            pltpu.VMEM((3, depth, rows, wide), f32),
            pltpu.VMEM((2, sects, 2, depth, rows, columns), f32),
            pltpu.VMEM((2, sects, 2, depth, rows, columns), f32),
            pltpu.VMEM((sects, depth, rows, columns), f32),
            pltpu.VMEM((sects, depth, 3 * rows, columns), f32),
            dma((6,)),
            dma((2, 4)),
            dma((2, 4)),
            dma((2,)),
            dma((2,)),
            dma((2, 4)),
            dma((2, 4)),
            dma((2, sects)),
            dma((2, sects)),
            dma((sects, 3)),
            dma((sects, 3)),
        ],
        compiler_params=pltpu.CompilerParams(collective_id=0, has_side_effects=True),
        name="coupled",
    )(zonal, merid, height, sea, flags, conc, level_kappa, react, absorb, light)


def solution(mesh):
    placed = (
        P("sect", "tile", None),
        P("sect", "tile", None),
        P("sect", "tile", None),
        P(),
        P("tile", None),
        P(None, "tile", "sect"),
        P(None, None, "tile", "sect"),
        P(),
        P(),
        P(),
    )
    return jax.shard_map(
        functools.partial(body, mesh.shape["sect"], mesh.shape["tile"]),
        mesh=mesh,
        in_specs=placed,
        out_specs=(
            P(None, None, "tile", "sect"),
            P("sect", "tile", None),
            P("sect", "tile", None),
            P("sect", "tile", None),
        ),
        check_vma=False,
    )
```

time: 118 us -> 28.7 us (0.24)
  starting transfers between devices: 52.9 us -> 0 us
  Pallas kernels: 0 us -> 24 us
  waiting for transfers between devices: 23.8 us -> 0 us
  local copies, waits for them, and re-layouts: 22.7 us -> 3.68 us
  other arithmetic: 14.9 us -> 0 us
    ppermute x24 -> x0, starting transfers between devices: 43.1 us -> none  [the longest x12 38.1 us: padded_2(): lax.ppermute(head, axis, [((i + 1) % count, i) for i in range(count)])]
    pallas_call x0 -> x1, Pallas kernels: none -> 24 us  [body(): pl.pallas_call(functools.partial(kernel, sects, tiles), out_shape=[jax.Sh...]
    ppermute x24 -> x0, waiting for transfers between devices: 13.6 us -> none  [the longest x12 9.59 us: padded_2(): lax.ppermute(tail, axis, [(i, (i + 1) % count) for i in range(count)])]
    all_to_all x3 -> x0, waiting for transfers between devices: 10.3 us -> none  [the longest x2 5.67 us: body(): lax.all_to_all(jnp.stack([zonal_mean, merid_mean, kappa_rows]), 'sect', s...]
    all_to_all x3 -> x0, starting transfers between devices: 9.8 us -> none  [the longest x2 6.55 us: body(): lax.all_to_all(jnp.stack([zonal_mean, merid_mean, kappa_rows]), 'sect', s...]
    unnamed x33 -> x10, local copies, waits for them, and re-layouts: 12.3 us -> 3.68 us
    unnamed x2 -> x0, other arithmetic: 6.67 us -> none
    slice x67 -> x0, local copies, waits for them, and re-layouts: 6.25 us -> none  [the longest x32 2.38 us: along_x(): return 0.5 * (jnp.roll(field, -1, 2) - jnp.roll(field, 1, 2))]
  transfers between devices with their start and end apart: 27 -> 0, of which waited for: 12 -> 0; matrix products, arithmetic and copies ran while one was open for 18% -> 0% of each run, Pallas kernels for 0% -> 0%
where the time goes in v1:
time: 28.7 us; the launch traced here: 28.3 us
  Pallas kernels  24 us (84%)
  local copies, waits for them, and re-layouts  3.68 us (13%)
  between operations  0.65 us (2%)
    pallas_call x1, Pallas kernels, body(): pl.pallas_call(functools.partial(kernel, sects, tiles), out_shape=[jax.Sh...  24 us
    unnamed x10, local copies, waits for them, and re-layouts  3.68 us

profile of v1, /device:TPU:0, one launch (start us, length us, event | category | flops | bytes accessed | tf_op | source)
XLA Modules:
  0.0 28.3 jit_solution(12752234074382968732)
XLA Ops:
  0.6 24.0 %coupled.1 = (f32[12,4,8,128]{3,2,1,0:T(8,128)}, f32[1,8,512]{2,1,0:T(8,128)}, f32[1,8,512]{2,1,0:T(8,128)}, f32[1,8,512]{2,1,0:T(8,128)}) custom-call(f32[1,8,512]{2,1,0:T(8,128)} %zonal_in.1, f32[1,8,512]{2,1,0:T(8,128)} %merid_in.1, f32[1,8,512]{2,1,0:T(8,128)} %height_in.1, s32[8,512]{1,0:T(8,128)} %sea_in.1, s32[4,8,128]{2,1,0:T(8,128)} %flags_in.1, ...), custom_call_target="tpu_custom_call" | custom-call | tf_op jit(solution)/shard_map/coupled/pallas_call | solution.py:471
  24.6 0.0 copy-start.2
  24.6 1.6 %copy.18 = f32[12,4,8,128]{3,2,1,0:T(8,128)} copy(f32[12,4,8,128]{3,2,1,0:T(8,128)} %get-tuple-element.8) | data formatting | bytes 393216
  26.2 0.0 copy-done.2
  26.2 0.0 copy-start.1
  26.2 0.6 %copy.19 = f32[1,8,512]{2,1,0:T(8,128)} copy(f32[1,8,512]{2,1,0:T(8,128)S(1)} %copy-done.2) | data formatting | bytes 32768
  26.9 0.1 copy-done.1
  27.0 0.0 copy-start
  27.0 0.6 %copy.20 = f32[1,8,512]{2,1,0:T(8,128)} copy(f32[1,8,512]{2,1,0:T(8,128)S(1)} %copy-done.1) | data formatting | bytes 32768
  27.6 0.1 copy-done
  27.7 0.6 %copy.21 = f32[1,8,512]{2,1,0:T(8,128)} copy(f32[1,8,512]{2,1,0:T(8,128)S(1)} %copy-done) | data formatting | bytes 32768
Async XLA Ops:
  24.6 1.6 %copy-start.2 = (f32[1,8,512]{2,1,0:T(8,128)S(1)}, f32[1,8,512]{2,1,0:T(8,128)}, u32[]{:S(2)}) copy-start(f32[1,8,512]{2,1,0:T(8,128)} %get-tuple-element.9) | copy-start | bytes 49156
  26.2 0.7 %copy-start.1 = (f32[1,8,512]{2,1,0:T(8,128)S(1)}, f32[1,8,512]{2,1,0:T(8,128)}, u32[]{:S(2)}) copy-start(f32[1,8,512]{2,1,0:T(8,128)} %get-tuple-element.10) | copy-start | bytes 49156
  27.0 0.7 %copy-start = (f32[1,8,512]{2,1,0:T(8,128)S(1)}, f32[1,8,512]{2,1,0:T(8,128)}, u32[]{:S(2)}) copy-start(f32[1,8,512]{2,1,0:T(8,128)} %get-tuple-element.11) | copy-start | bytes 49156

commit v2 on v1

--- a/solution.py
+++ b/solution.py
@@ -80,14 +80,18 @@
     sea_in,
     flags_in,
     conc_in,
+    kappa_hbm,
+    react_hbm,
+    absorb_hbm,
+    light_hbm,
+    conc_out,
+    zonal_out,
+    merid_out,
+    height_out,
     kappa_in,
     react_in,
     absorb_in,
     light_in,
-    conc_out,
-    zonal_out,
-    merid_out,
-    height_out,
     ocean,
     sea,
     flags,
@@ -152,6 +156,17 @@
         pltpu.make_async_copy(field, ocean.at[0, f, :, slot(0)], local_sem.at[3 + f])
         for f, field in enumerate(fields_in)
     ]
+    scalars = [
+        pltpu.make_async_copy(src, dst, local_sem.at[6 + i])
+        for i, (src, dst) in enumerate(
+            (
+                (react_hbm, react_in),
+                (absorb_hbm, absorb_in),
+                (kappa_hbm, kappa_in),
+                (light_hbm, light_in),
+            )
+        )
+    ]
     barrier = pltpu.get_barrier_semaphore()
     peers = [(o, d) for o in range(sects) for d in (1, -1, 0) if (o, d) != (0, 0)]
     for o, d in peers:
@@ -161,7 +176,7 @@
             device_id=(sect_at(o), steps_t[d]),
             device_id_type=pl.DeviceIdType.MESH,
         )
-    for copy in local:
+    for copy in scalars + local:
         copy.start()
     pl.semaphore_wait(barrier, len(peers))
 
@@ -195,7 +210,7 @@
     lane = lax.broadcasted_iota(jnp.int32, (rows, columns), 1)
     row = lax.broadcasted_iota(jnp.int32, (rows, columns), 0)
 
-    for copy in local[:3]:
+    for copy in scalars + local[:3]:
         copy.wait()
     own_columns = pl.ds(pl.multiple_of(me_s * columns, LANES), columns)
     sea_cols = sea[slot(0), own_columns]
@@ -456,6 +471,17 @@
         copy.wait_send()
 
 
+def put_out(*refs):
+    copies = [
+        pltpu.make_async_copy(src, dst, refs[8].at[i])
+        for i, (src, dst) in enumerate(zip(refs[:4], refs[4:8]))
+    ]
+    for copy in copies:
+        copy.start()
+    for copy in copies:
+        copy.wait()
+
+
 def body(sects, tiles, zonal, merid, height, level_kappa, sea, flags, conc, react, absorb, light):
     tracers, levels, rows, columns = conc.shape
     depth, _, wide = zonal.shape
@@ -466,19 +492,22 @@
     f32 = jnp.float32
     dma = pltpu.SemaphoreType.DMA
     any_space = pl.BlockSpec(memory_space=pl.ANY)
-    smem = pl.BlockSpec(memory_space=pltpu.SMEM)
     vmem = pl.BlockSpec(memory_space=pltpu.VMEM)
-    return pl.pallas_call(
+    results = pl.pallas_call(
         functools.partial(kernel, sects, tiles),
         out_shape=[
-            jax.ShapeDtypeStruct(conc.shape, f32),
-            jax.ShapeDtypeStruct(zonal.shape, f32),
-            jax.ShapeDtypeStruct(merid.shape, f32),
-            jax.ShapeDtypeStruct(height.shape, f32),
+            pltpu.VMEM(conc.shape, f32),
+            pltpu.VMEM(zonal.shape, f32),
+            pltpu.VMEM(merid.shape, f32),
+            pltpu.VMEM(height.shape, f32),
         ],
-        in_specs=[any_space] * 6 + [smem] * 4,
+        in_specs=[pl.BlockSpec(memory_space=pltpu.HBM)] * 10,
         out_specs=[vmem] * 4,
         scratch_shapes=[
+            pltpu.SMEM(level_kappa.shape, f32),
+            pltpu.SMEM(react.shape, f32),
+            pltpu.SMEM(absorb.shape, f32),
+            pltpu.SMEM(light.shape, f32),
             pltpu.VMEM((2, 3, depth, 3 * rows, wide), f32),
             pltpu.VMEM((3 * rows, wide), jnp.int32),
             pltpu.VMEM(flags.shape, jnp.int32),
@@ -495,7 +524,7 @@
             pltpu.VMEM((2, sects, 2, depth, rows, columns), f32),
             pltpu.VMEM((sects, depth, rows, columns), f32),
             pltpu.VMEM((sects, depth, 3 * rows, columns), f32),
-            dma((6,)),
+            dma((10,)),
             dma((2, 4)),
             dma((2, 4)),
             dma((2,)),
@@ -510,6 +539,14 @@
         compiler_params=pltpu.CompilerParams(collective_id=0, has_side_effects=True),
         name="coupled",
     )(zonal, merid, height, sea, flags, conc, level_kappa, react, absorb, light)
+    return pl.pallas_call(
+        put_out,
+        out_shape=[jax.ShapeDtypeStruct(r.shape, f32) for r in results],
+        in_specs=[vmem] * 4,
+        out_specs=[any_space] * 4,
+        scratch_shapes=[dma((4,))],
+        name="put_out",
+    )(*[pltpu.with_memory_space_constraint(r, pltpu.VMEM) for r in results])
 
 
 def solution(mesh):

time: 28.7 us -> 24 us (0.84)
  local copies, waits for them, and re-layouts: 3.68 us -> 0 us
  Pallas kernels: 24 us -> 23.2 us
    unnamed x10 -> x0, local copies, waits for them, and re-layouts: 3.68 us -> none
    pallas_call x1 -> x2, Pallas kernels: 24 us -> 23.2 us  [the longest x1 22.5 us: body(): pl.pallas_call(functools.partial(kernel, sects, tiles), out_shape=[pltpu....]
where the time goes in v2:
time: 24 us; the launch traced here: 23.9 us
  Pallas kernels  23.2 us (97%)
  between operations  0.64 us (3%)
    pallas_call x1, Pallas kernels, body(): pl.pallas_call(functools.partial(kernel, sects, tiles), out_shape=[pltpu....  22.5 us
    pallas_call x1, Pallas kernels, body(): pl.pallas_call(put_out, out_shape=[jax.ShapeDtypeStruct(r.shape, f32) for...  0.72 us

profile of v2, /device:TPU:0, one launch (start us, length us, event | category | flops | bytes accessed | tf_op | source)
XLA Modules:
  0.0 23.9 jit_solution(8158237894192600614)
XLA Ops:
  0.6 22.5 %coupled.1 = (f32[12,4,8,128]{3,2,1,0:T(8,128)S(1)}, f32[1,8,512]{2,1,0:T(8,128)S(1)}, f32[1,8,512]{2,1,0:T(8,128)S(1)}, f32[1,8,512]{2,1,0:T(8,128)S(1)}) custom-call(f32[1,8,512]{2,1,0:T(8,128)} %zonal_in.1, f32[1,8,512]{2,1,0:T(8,128)} %merid_in.1, f32[1,8,512]{2,1,0:T(8,128)} %height_in.1, s32[8,512]{1,0:T(8,128)} %sea_in.1, s32[4,8,128]{2,1,0:T(8,128)} %flags_in.1, ...), custom_call_target="tpu_custom_call" | custom-call | tf_op jit(solution)/shard_map/coupled/pallas_call | solution.py:496
  23.2 0.7 %put_out.1 = (f32[12,4,8,128]{3,2,1,0:T(8,128)}, f32[1,8,512]{2,1,0:T(8,128)}, f32[1,8,512]{2,1,0:T(8,128)}, f32[1,8,512]{2,1,0:T(8,128)}) custom-call(f32[12,4,8,128]{3,2,1,0:T(8,128)S(1)} %get-tuple-element.8.refs_0_, f32[1,8,512]{2,1,0:T(8,128)S(1)} %get-tuple-element.9.refs_1_, f32[1,8,512]{2,1,0:T(8,128)S(1)} %get-tuple-element.10.refs_2_, ...), custom_call_target="tpu_custom_call" | custom-call | tf_op jit(solution)/shard_map/put_out/pallas_call | solution.py:542

commit v3 on v2

--- a/solution.py
+++ b/solution.py
@@ -122,6 +122,7 @@
     mean_rsem,
     heat_ssem,
     heat_rsem,
+    known_sem,
 ):
     me_s = lax.axis_index("sect")
     me_t = lax.axis_index("tile")
@@ -133,6 +134,24 @@
 
     def sect_at(offset):
         return lax.rem(me_s + offset, sects)
+
+    def flipped(bit):
+        step = 1 << bit
+        return me_s + step - 2 * step * lax.rem(me_s // step, 2)
+
+    def tell(bit):
+        pl.semaphore_signal(
+            known_sem.at[bit],
+            inc=1,
+            device_id=(flipped(bit), me_t),
+            device_id_type=pl.DeviceIdType.MESH,
+        )
+
+    def hear_of_all():
+        for b in range(bits - 1):
+            pl.semaphore_wait(known_sem.at[b], 1)
+            if b + 1 < bits - 1:
+                tell(b + 1)
 
     def remote(src, dst, send, recv, to_s, to_t):
         return pltpu.make_async_remote_copy(
@@ -168,17 +187,15 @@
         )
     ]
     barrier = pltpu.get_barrier_semaphore()
-    peers = [(o, d) for o in range(sects) for d in (1, -1, 0) if (o, d) != (0, 0)]
-    for o, d in peers:
+    bits = sects.bit_length() - 1
+    greeted = [(me_s, above), (me_s, below)] + [(flipped(b), me_t) for b in range(bits)]
+    for peer in greeted:
         pl.semaphore_signal(
-            barrier,
-            inc=1,
-            device_id=(sect_at(o), steps_t[d]),
-            device_id_type=pl.DeviceIdType.MESH,
+            barrier, inc=1, device_id=peer, device_id_type=pl.DeviceIdType.MESH
         )
     for copy in scalars + local:
         copy.start()
-    pl.semaphore_wait(barrier, len(peers))
+    pl.semaphore_wait(barrier, len(greeted))
 
     first = []
     for i, d in enumerate((1, -1)):
@@ -205,6 +222,8 @@
         )
     for copy in first:
         copy.start()
+    if bits > 1:
+        tell(0)
     sent = list(first)
 
     lane = lax.broadcasted_iota(jnp.int32, (rows, columns), 1)
@@ -252,6 +271,8 @@
         for p in range(len(to_east)):
             cols_send[turn, 0, p] = to_east[p]
             cols_send[turn, 1, p] = to_west[p]
+        if turn == 0:
+            hear_of_all()
         copies = []
         for i, d in enumerate((1, -1)):
             copies.append(
@@ -442,10 +463,6 @@
         for k, value in enumerate(tracer_column(terms, i)):
             conc[i, k] = value
     halo1, cells1 = react_and_send(1, False)
-    for copy in halo1:
-        copy.wait_recv()
-    shift_cells(1, cells1)
-
     for copy in state:
         copy.wait_recv()
     for copy in heats:
@@ -461,6 +478,9 @@
         merid_out[l] = m
         height_out[l] = h
     got = send_means(1, means)
+    for copy in halo1:
+        copy.wait_recv()
+    shift_cells(1, cells1)
     for copy in got:
         copy.wait_recv()
     terms = column_terms(1)
@@ -485,7 +505,7 @@
 def body(sects, tiles, zonal, merid, height, level_kappa, sea, flags, conc, react, absorb, light):
     tracers, levels, rows, columns = conc.shape
     depth, _, wide = zonal.shape
-    assert rows >= 2 * STEPS and columns % LANES == 0 and INTERVALS == 2
+    assert sects & (sects - 1) == 0 and rows >= 2 * STEPS and columns % LANES == 0 and INTERVALS == 2
     cells = (tracers + 1) * levels
     packs = pl.cdiv(cells, LANES)
     padded = pl.cdiv(cells, 8) * 8
@@ -535,6 +555,7 @@
             dma((2, sects)),
             dma((sects, 3)),
             dma((sects, 3)),
+            pltpu.SemaphoreType.REGULAR((max(sects.bit_length() - 2, 1),)),
         ],
         compiler_params=pltpu.CompilerParams(collective_id=0, has_side_effects=True),
         name="coupled",

time: 24 us -> 22.6 us (0.942)
  Pallas kernels: 23.2 us -> 21.8 us
    pallas_call x1, Pallas kernels: 22.5 us -> 21.1 us  [body(): pl.pallas_call(functools.partial(kernel, sects, tiles), out_shape=[pltpu....]
where the time goes in v3:
time: 22.6 us; the launch traced here: 22.5 us
  Pallas kernels  21.8 us (96%)
  between operations  0.64 us (3%)
    pallas_call x1, Pallas kernels, body(): pl.pallas_call(functools.partial(kernel, sects, tiles), out_shape=[pltpu....  21.1 us
    pallas_call x1, Pallas kernels, body(): pl.pallas_call(put_out, out_shape=[jax.ShapeDtypeStruct(r.shape, f32) for...  0.72 us

profile of v3, /device:TPU:0, one launch (start us, length us, event | category | flops | bytes accessed | tf_op | source)
XLA Modules:
  0.0 22.5 jit_solution(12673590682052975940)
XLA Ops:
  0.6 21.1 %coupled.1 = (f32[12,4,8,128]{3,2,1,0:T(8,128)S(1)}, f32[1,8,512]{2,1,0:T(8,128)S(1)}, f32[1,8,512]{2,1,0:T(8,128)S(1)}, f32[1,8,512]{2,1,0:T(8,128)S(1)}) custom-call(f32[1,8,512]{2,1,0:T(8,128)} %zonal_in.1, f32[1,8,512]{2,1,0:T(8,128)} %merid_in.1, f32[1,8,512]{2,1,0:T(8,128)} %height_in.1, s32[8,512]{1,0:T(8,128)} %sea_in.1, s32[4,8,128]{2,1,0:T(8,128)} %flags_in.1, ...), custom_call_target="tpu_custom_call" | custom-call | tf_op jit(solution)/shard_map/coupled/pallas_call | solution.py:516
  21.8 0.7 %put_out.1 = (f32[12,4,8,128]{3,2,1,0:T(8,128)}, f32[1,8,512]{2,1,0:T(8,128)}, f32[1,8,512]{2,1,0:T(8,128)}, f32[1,8,512]{2,1,0:T(8,128)}) custom-call(f32[12,4,8,128]{3,2,1,0:T(8,128)S(1)} %get-tuple-element.8.refs_0_, f32[1,8,512]{2,1,0:T(8,128)S(1)} %get-tuple-element.9.refs_1_, f32[1,8,512]{2,1,0:T(8,128)S(1)} %get-tuple-element.10.refs_2_, ...), custom_call_target="tpu_custom_call" | custom-call | tf_op jit(solution)/shard_map/put_out/pallas_call | solution.py:563

commit v4 on v3

--- a/solution.py
+++ b/solution.py
@@ -21,7 +21,7 @@
 LANES = 128
 
 
-def ocean_steps(zonal, merid, height, wet, forcing, rows):
+def ocean_steps(zonal, merid, height, wet, heating, rows):
     tall, wide = zonal.shape
 
     def east(a):
@@ -39,32 +39,21 @@
     own = slice(rows, 2 * rows)
     zonal_sum = jnp.zeros((rows, wide), jnp.float32)
     merid_sum = jnp.zeros((rows, wide), jnp.float32)
-    for _ in range(STEPS):
+    for step in range(STEPS):
         ze, zw, zn, zs = east(zonal), west(zonal), north(zonal), south(zonal)
         me, mw, mn, ms = east(merid), west(merid), north(merid), south(merid)
         height = height - (0.5 * time_step) * ((ze - zw) + (mn - ms))
-        if forcing is not None:
-            height = height + (time_step * heat_coupling) * forcing
         zonal_lap = zn + zs + ze + zw - 4.0 * zonal
         merid_lap = mn + ms + me + mw - 4.0 * merid
-        zonal_new = wet * (
-            zonal
-            + time_step
-            * (
-                coriolis * merid
-                - (0.5 * gravity) * (east(height) - west(height))
-                + viscosity * zonal_lap
-            )
-        )
-        merid_new = wet * (
-            merid
-            + time_step
-            * (
-                -coriolis * zonal
-                - (0.5 * gravity) * (north(height) - south(height))
-                + viscosity * merid_lap
-            )
-        )
+        zonal_part = zonal + time_step * (coriolis * merid + viscosity * zonal_lap)
+        merid_part = merid + time_step * (-coriolis * zonal + viscosity * merid_lap)
+        if heating is not None:
+            if step == 0:
+                forced = (time_step * heat_coupling) * heating()
+            height = height + forced
+        slope = 0.5 * gravity * time_step
+        zonal_new = wet * (zonal_part - slope * (east(height) - west(height)))
+        merid_new = wet * (merid_part - slope * (north(height) - south(height)))
         zonal, merid = zonal_new, merid_new
         zonal_sum = zonal_sum + zonal[own]
         merid_sum = merid_sum + merid[own]
@@ -236,7 +225,7 @@
     wet_cols = sea_cols.astype(jnp.float32)
     is_wet = sea_cols == 1
 
-    def react_and_send(turn, heated):
+    def react_and_pack(turn, heated):
         names = tracers + (1 if heated else 0)
         cells = names * levels
         to_east = [jnp.zeros((rows, columns), jnp.float32) for _ in range(pl.cdiv(cells, LANES))]
@@ -271,8 +260,6 @@
         for p in range(len(to_east)):
             cols_send[turn, 0, p] = to_east[p]
             cols_send[turn, 1, p] = to_west[p]
-        if turn == 0:
-            hear_of_all()
         copies = []
         for i, d in enumerate((1, -1)):
             copies.append(
@@ -295,9 +282,6 @@
                     me_t,
                 )
             )
-        for copy in copies:
-            copy.start()
-        sent.extend(copies)
         return copies, cells
 
     def shift_cells(turn, cells):
@@ -395,11 +379,15 @@
             partial[k] = partial[k] + terms[k]["upper"] * partial[k + 1]
         return partial
 
-    halo0, cells0 = react_and_send(0, True)
+    halo0, cells0 = react_and_pack(0, True)
     for copy in local[3:]:
         copy.wait()
     for copy in first:
         copy.wait_recv()
+    hear_of_all()
+    for copy in halo0:
+        copy.start()
+    sent.extend(halo0)
     wet = sea[...].astype(jnp.float32)
     means = []
     for l in range(depth):
@@ -462,16 +450,23 @@
     for i in range(tracers):
         for k, value in enumerate(tracer_column(terms, i)):
             conc[i, k] = value
-    halo1, cells1 = react_and_send(1, False)
+    halo1, cells1 = react_and_pack(1, False)
+    for copy in halo1:
+        copy.start()
+    sent.extend(halo1)
     for copy in state:
         copy.wait_recv()
-    for copy in heats:
-        copy.wait_recv()
+
+    def heating(l):
+        if l == 0:
+            for copy in heats:
+                copy.wait_recv()
+        return jnp.concatenate([heat_recv[s, l] for s in range(sects)], axis=1)
+
     means = []
     for l in range(depth):
-        forcing = jnp.concatenate([heat_recv[s, l] for s in range(sects)], axis=1)
         z, m, h, zm, mm = ocean_steps(
-            ocean[1, 0, l], ocean[1, 1, l], ocean[1, 2, l], wet, forcing, rows
+            ocean[1, 0, l], ocean[1, 1, l], ocean[1, 2, l], wet, functools.partial(heating, l), rows
         )
         means.append((zm, mm))
         zonal_out[l] = z

time: 22.6 us -> 22.5 us (level)
  no operation moved by 1% of the time
where the time goes in v4:
time: 22.5 us; the launch traced here: 22.4 us
  Pallas kernels  21.7 us (96%)
  between operations  0.64 us (3%)
    pallas_call x1, Pallas kernels, body(): pl.pallas_call(functools.partial(kernel, sects, tiles), out_shape=[pltpu....  21 us
    pallas_call x1, Pallas kernels, body(): pl.pallas_call(put_out, out_shape=[jax.ShapeDtypeStruct(r.shape, f32) for...  0.72 us

profile of v4, /device:TPU:0, one launch (start us, length us, event | category | flops | bytes accessed | tf_op | source)
XLA Modules:
  0.0 22.4 jit_solution(6673957866832800961)
XLA Ops:
  0.6 21.0 %coupled.1 = (f32[12,4,8,128]{3,2,1,0:T(8,128)S(1)}, f32[1,8,512]{2,1,0:T(8,128)S(1)}, f32[1,8,512]{2,1,0:T(8,128)S(1)}, f32[1,8,512]{2,1,0:T(8,128)S(1)}) custom-call(f32[1,8,512]{2,1,0:T(8,128)} %zonal_in.1, f32[1,8,512]{2,1,0:T(8,128)} %merid_in.1, f32[1,8,512]{2,1,0:T(8,128)} %height_in.1, s32[8,512]{1,0:T(8,128)} %sea_in.1, s32[4,8,128]{2,1,0:T(8,128)} %flags_in.1, ...), custom_call_target="tpu_custom_call" | custom-call | tf_op jit(solution)/shard_map/coupled/pallas_call | solution.py:511
  21.7 0.7 %put_out.1 = (f32[12,4,8,128]{3,2,1,0:T(8,128)}, f32[1,8,512]{2,1,0:T(8,128)}, f32[1,8,512]{2,1,0:T(8,128)}, f32[1,8,512]{2,1,0:T(8,128)}) custom-call(f32[12,4,8,128]{3,2,1,0:T(8,128)S(1)} %get-tuple-element.8.refs_0_, f32[1,8,512]{2,1,0:T(8,128)S(1)} %get-tuple-element.9.refs_1_, f32[1,8,512]{2,1,0:T(8,128)S(1)} %get-tuple-element.10.refs_2_, ...), custom_call_target="tpu_custom_call" | custom-call | tf_op jit(solution)/shard_map/put_out/pallas_call | solution.py:558
